TPU v7x, 32 devices: a whole 2x2x4 slice. The times are simulated.
32 devices in a mesh: parts: 2 (over x), ctx: 4 (over z), branch: 4 (over y, core).
Axes of the slice: x: 2, y: 2, z: 4, core: 2. Of those that a mesh axis runs over, the one named last changes fastest.
Arguments:
- prefix_kv: bfloat16 [2, 8192, 1024], P(None, ('parts', 'ctx')), parts along dimension 1
- queries: bfloat16 [512, 8192], P(('parts', 'ctx', 'branch')), parts along dimension 0
- new_kv: bfloat16 [2, 512, 1024], P(None, ('parts', 'ctx', 'branch')), parts along dimension 1, may hold values from -6 to 6
- suffix_kv: bfloat16 [2, 512, 64, 1024], P(None, ('parts', 'ctx', 'branch')), parts along dimension 1, may hold values from -6 to 6
- suffix_len: int32 [512], P(('parts', 'ctx', 'branch')), parts along dimension 0, may hold values from 1 to 64, as said below
- node_kv: bfloat16 [2, 8, 128, 1024], P(None, ('parts', 'branch')), parts along dimension 1, may hold values from -6 to 6
- node_len: int32 [8], P('parts'), parts along dimension 0, may hold values from 1 to 128, as said below
- parent: int32 [8], P('parts'), parts along dimension 0, may hold values from -1 to 2, as said below
- leaf: int32 [512], P(('parts', 'ctx', 'branch')), parts along dimension 0, may hold values from 0 to 3
Outputs:
- context: bfloat16 [512, 8192], P(('parts', 'ctx', 'branch')), parts along dimension 0
There are 2 independent parts, one for each index of `parts`. A program takes and returns all parts, laid end to end along the dimension named above; each array names one. Nothing has to cross between parts.
Inputs may be any that keep to these rules, and one draw needn't show every extreme that they name: `suffix_len`: live tokens stand first in a rollout's suffix; some rollout has all 64. `node_len`: live tokens stand first in a node; some node has all 128. parent[n] is -1 or a node below n; parent[0] is -1.
All inputs are finite; a program needn't handle non-finite values.
Results may differ from a plain program's by a relative error of at most 0.0055.
Values may be sent and summed in bfloat16 or wider, within the bound.
A program may use at most 128 MiB of HBM per device.

v0:
```python
import math
import jax
import jax.numpy as jnp
from jax import lax
from jax.sharding import PartitionSpec as P

HEADS = 64
KV_HEADS = 8
HEAD_DIM = 128
NODE_LEN = 128


def attend(query_block, key_rows, value_rows, live_mask):
    scores = jnp.einsum("bhgd,thd->bhgt", query_block, key_rows, preferred_element_type=jnp.float32)
    scores = scores * query_block.shape[-1] ** (-0.5)
    if live_mask is not None:
        scores = jnp.where(live_mask[:, None, None, :], scores, -jnp.inf)
    maxima = jnp.max(scores, axis=-1)
    anchor = jnp.where(jnp.isfinite(maxima), maxima, 0.0)
    weights = jnp.exp(scores - anchor[..., None])
    totals = jnp.sum(weights, axis=-1)
    mixed = jnp.einsum(
        "bhgt,thd->bhgd",
        weights.astype(jnp.bfloat16),
        value_rows,
        preferred_element_type=jnp.float32,
    )
    return (mixed, maxima, totals)


def combine(first, second):
    mixed_a, maxima_a, totals_a = first
    mixed_b, maxima_b, totals_b = second
    maxima = jnp.maximum(maxima_a, maxima_b)
    anchor = jnp.where(jnp.isfinite(maxima), maxima, 0.0)
    scale_a = jnp.exp(maxima_a - anchor)
    scale_b = jnp.exp(maxima_b - anchor)
    mixed = mixed_a * scale_a[..., None] + mixed_b * scale_b[..., None]
    return (mixed, maxima, totals_a * scale_a + totals_b * scale_b)


def merge_parts(back_mixed, back_maxima, back_totals, ctx_size, rollouts, group):
    back_mixed = back_mixed.reshape(ctx_size, rollouts, KV_HEADS, group, HEAD_DIM)
    back_maxima = back_maxima.reshape(ctx_size, rollouts, KV_HEADS, group)
    back_totals = back_totals.reshape(ctx_size, rollouts, KV_HEADS, group)
    peak = jnp.max(back_maxima, axis=0)
    factors = jnp.exp(back_maxima - peak[None])
    return (
        jnp.sum(back_mixed * factors[..., None], axis=0),
        peak,
        jnp.sum(back_totals * factors, axis=0),
    )


def on_device(prefix_kv, queries, new_kv, suffix_kv, suffix_len, node_kv, node_len, parent, leaf):
    rollouts = queries.shape[0]
    group = HEADS // KV_HEADS
    inverse_root = HEAD_DIM ** (-0.5)
    query_heads = queries.reshape(rollouts, KV_HEADS, group, HEAD_DIM)
    prefix_keys = prefix_kv[0].reshape(-1, KV_HEADS, HEAD_DIM)
    prefix_values = prefix_kv[1].reshape(-1, KV_HEADS, HEAD_DIM)
    node_count = node_len.shape[0]
    node_ids = jnp.arange(node_count, dtype=jnp.int32)
    token_ids = jnp.arange(NODE_LEN, dtype=jnp.int32)
    ctx_size = lax.axis_size("ctx")
    query_rows = lax.all_gather(queries, "ctx", axis=0, tiled=True)
    count = query_rows.shape[0]
    width = math.gcd(count, 16)
    blocks = query_rows.reshape(count // width, width, KV_HEADS, group, HEAD_DIM)

    def one_block(block_rows):
        return attend(block_rows, prefix_keys, prefix_values, None)

    mixed, maxima, totals = lax.map(one_block, blocks)
    fresh = (
        mixed.reshape(count, KV_HEADS, group, HEAD_DIM),
        maxima.reshape(count, KV_HEADS, group),
        totals.reshape(count, KV_HEADS, group),
    )
    held_mixed, held_maxima, held_totals = tuple((made for made in fresh))
    back_mixed, back_maxima, back_totals = (
        lax.all_to_all(held_mixed, "ctx", split_axis=0, concat_axis=0, tiled=True),
        lax.all_to_all(held_maxima, "ctx", split_axis=0, concat_axis=0, tiled=True),
        lax.all_to_all(held_totals, "ctx", split_axis=0, concat_axis=0, tiled=True),
    )
    prefix_state = merge_parts(back_mixed, back_maxima, back_totals, ctx_size, rollouts, group)

    def climb(turn_index, carry):
        current, member = carry
        matched = current[:, None] == node_ids[None, :]
        member = member | matched
        lifted = jnp.sum(jnp.where(matched, parent[None, :], 0), axis=1)
        current = jnp.where(current >= 0, lifted, -1)
        return (current, member)

    start_member = jnp.zeros((leaf.shape[0], node_count), dtype=bool)
    ignored, member = lax.fori_loop(0, node_count, climb, (leaf, start_member))
    shard_piece = lax.all_gather(node_kv, "branch", axis=1, tiled=True)
    count = shard_piece.shape[1]
    live_mask = (member[:, :, None] & (token_ids[None, :] < node_len[:, None])[None, :, :]).reshape(
        member.shape[0], count * NODE_LEN
    )
    key_rows = shard_piece[0].reshape(count * NODE_LEN, KV_HEADS, HEAD_DIM)
    value_rows = shard_piece[1].reshape(count * NODE_LEN, KV_HEADS, HEAD_DIM)
    node_state = combine(
        (
            jnp.zeros((rollouts, KV_HEADS, group, HEAD_DIM), jnp.float32),
            jnp.full((rollouts, KV_HEADS, group), -jnp.inf, jnp.float32),
            jnp.zeros((rollouts, KV_HEADS, group), jnp.float32),
        ),
        attend(query_heads, key_rows, value_rows, live_mask),
    )
    front_state = combine(prefix_state, node_state)
    suffix_keys = suffix_kv[0].reshape(rollouts, -1, KV_HEADS, HEAD_DIM)
    suffix_values = suffix_kv[1].reshape(rollouts, -1, KV_HEADS, HEAD_DIM)
    suffix_scores = (
        jnp.einsum("rhgd,rshd->rhgs", query_heads, suffix_keys, preferred_element_type=jnp.float32)
        * inverse_root
    )
    positions = jnp.arange(suffix_keys.shape[1], dtype=jnp.int32)
    suffix_live = positions[None, :] < suffix_len[:, None]
    suffix_scores = jnp.where(suffix_live[:, None, None, :], suffix_scores, -jnp.inf)
    suffix_peak = jnp.max(suffix_scores, axis=-1)
    suffix_weights = jnp.exp(suffix_scores - suffix_peak[..., None])
    suffix_mixed = jnp.einsum(
        "rhgs,rshd->rhgd",
        suffix_weights.astype(jnp.bfloat16),
        suffix_values,
        preferred_element_type=jnp.float32,
    )
    suffix_state = (suffix_mixed, suffix_peak, jnp.sum(suffix_weights, axis=-1))
    fresh_keys = new_kv[0].reshape(rollouts, KV_HEADS, HEAD_DIM)
    fresh_values = new_kv[1].reshape(rollouts, KV_HEADS, HEAD_DIM).astype(jnp.float32)
    fresh_scores = (
        jnp.einsum("rhgd,rhd->rhg", query_heads, fresh_keys, preferred_element_type=jnp.float32)
        * inverse_root
    )
    fresh_mixed = jnp.broadcast_to(
        fresh_values[:, :, None, :], (rollouts, KV_HEADS, group, HEAD_DIM)
    )
    fresh_state = (fresh_mixed, fresh_scores, jnp.ones_like(fresh_scores))
    state = combine(combine(front_state, suffix_state), fresh_state)
    context = state[0] / state[2][..., None]
    return context.astype(jnp.bfloat16).reshape(rollouts, HEADS * HEAD_DIM)


def solution(mesh):
    return jax.shard_map(
        on_device,
        mesh=mesh,
        in_specs=(
            P(None, ("parts", "ctx"), None),
            P(("parts", "ctx", "branch"), None),
            P(None, ("parts", "ctx", "branch"), None),
            P(None, ("parts", "ctx", "branch"), None, None),
            P(("parts", "ctx", "branch")),
            P(None, ("parts", "branch"), None, None),
            P("parts"),
            P("parts"),
            P(("parts", "ctx", "branch")),
        ),
        out_specs=P(("parts", "ctx", "branch"), None),
        check_vma=False,
    )
```

profile of v0, /device:TPU:0, one launch (start us, length us, event | category | flops | bytes accessed | tf_op | source)
XLA Modules:
  0.0 144.7 jit_solution(16751887422370051576)
XLA Ops:
  8.0 4.0 %fusion.64 = (bf16[1,1024,1024]{2,1,0:T(8,128)(2,1)}, bf16[1,1024,1024]{2,1,0:T(8,128)(2,1)S(1)}) fusion(bf16[2,1024,1024]{2,1,0:T(8,128)(2,1)} %param.13), kind=kLoop, calls=%fused_computation.78 | loop fusion | bytes 8388608 | tf_op jit(solution)/shard_map/slice | solution.py:61
  12.0 2.6 %copy.184 = bf16[1,1024,1024]{1,2,0:T(8,128)(2,1)} copy(bf16[1,1024,1024]{2,1,0:T(8,128)(2,1)S(1)} %get-tuple-element.163) | data formatting | bytes 4194304
  14.6 3.0 %copy.125 = bf16[1024,8,128]{2,0,1:T(8,128)(2,1)S(1)} copy(bf16[1024,8,128]{0,2,1:T(8,128)(2,1)} %bitcast.128) | data formatting | bytes 4194304 | tf_op jit(solution)/shard_map/while | solution.py:74
  17.6 4.0 %copy.185 = bf16[1,1024,1024]{1,2,0:T(8,128)(2,1)} copy(bf16[1,1024,1024]{2,1,0:T(8,128)(2,1)} %get-tuple-element.162) | data formatting | bytes 4194304
  21.6 3.9 %copy.126 = bf16[1024,8,128]{2,0,1:T(8,128)(2,1)} copy(bf16[1024,8,128]{0,2,1:T(8,128)(2,1)} %bitcast.129) | data formatting | bytes 4194304 | tf_op jit(solution)/shard_map/while | solution.py:74
  26.0 13.6 %all-gather.3.cloned.1.call-done = bf16[64,8192]{1,0:T(8,128)(2,1)} async-done(((bf16[16,8192]{1,0:T(8,128)(2,1)}), bf16[64,8192]{1,0:T(8,128)(2,1)}) %all-gather.3.cloned.1.call-update) | async-done | bytes 1048592 | tf_op jit(solution)/shard_map/all_gather | solution.py:66
  39.6 1.5 %copy.190 = bf16[8,8,64,128]{3,2,1,0:T(8,128)(2,1)S(1)} copy(bf16[8,8,64,128]{3,1,2,0:T(8,128)(2,1)} %bitcast.141) | data formatting | bytes 2097152
  41.1 17.2 %while.27 = (s32[]{:T(128)}, f32[4,16,8,8,128]{4,3,2,1,0:T(8,128)}, f32[4,16,8,8]{3,2,1,0:T(8,128)S(1)}, f32[4,16,8,8]{3,2,1,0:T(8,128)}, bf16[4,16,8,8,128]{4,3...) while((s32[]{:T(128)}, f32[4,16,8,8,128]{4,3,2,1,0:T(8,128)}, ...), condition=%wide.region_3.4_spmd, body=%wide.region_0.3_spmd.sunk | while | flops 545259520 | bytes 27288692 | solution.py:74
  41.1 0.8 bitcast_reduce_fusion.2
  41.9 0.9 fusion.81
  43.5 1.0 fusion.80
  44.5 0.9 copy_dynamic-update-slice_fusion.5
  45.4 0.8 bitcast_reduce_fusion.2
  46.2 0.9 fusion.81
  47.9 1.0 fusion.80
  48.9 0.9 copy_dynamic-update-slice_fusion.5
  49.8 0.8 bitcast_reduce_fusion.2
  50.6 0.9 fusion.81
  52.2 1.0 fusion.80
  53.2 0.8 copy_dynamic-update-slice_fusion.5
  54.0 0.8 bitcast_reduce_fusion.2
  54.8 0.9 fusion.81
  56.4 1.0 fusion.80
  57.4 0.9 copy_dynamic-update-slice_fusion.5
  59.1 3.3 %all-to-all-start.1 = ((f32[4,1,1024]{2,1,0:T(1,128)}), f32[4,1,1024]{2,1,0:T(1,128)S(1)}, u32[]{:S(2)}, u32[]{:S(2)}) async-start(f32[4,1,1024]{2,1,0:T(1,128)} %reshape.165), calls=%async_computation.1 | async-start | bytes 32768 | tf_op jit(solution)/shard_map/all_to_all | solution.py:83
  62.4 5.0 %fusion.63 = (bf16[1,16,64,1024]{3,2,1,0:T(8,128)(2,1)}, bf16[1,16,64,1024]{3,2,1,0:T(8,128)(2,1)}) fusion(bf16[2,16,64,1024]{3,2,1,0:T(8,128)(2,1)} %param.16), kind=kLoop, calls=%fused_computation.77 | loop fusion | bytes 8388608 | tf_op jit(solution)/shard_map/slice | solution.py:115
  68.1 5.0 %all-to-all-start.2 = ((f32[4,1,1024]{2,1,0:T(1,128)}), f32[4,1,1024]{2,1,0:T(1,128)S(1)}, u32[]{:S(2)}, u32[]{:S(2)}) async-start(f32[4,1,1024]{2,1,0:T(1,128)} %reshape.167), calls=%async_computation.2 | async-start | bytes 32768 | tf_op jit(solution)/shard_map/all_to_all | solution.py:84
  73.3 2.2 %copy.195 = bf16[128,8,8,128]{3,2,1,0:T(8,128)(2,1)S(1)} copy(bf16[128,8,8,128]{3,1,2,0:T(8,128)(2,1)} %bitcast.131) | data formatting | bytes 4194304
  75.6 3.5 %copy.196 = bf16[128,8,8,128]{3,2,1,0:T(8,128)(2,1)} copy(bf16[128,8,8,128]{3,1,2,0:T(8,128)(2,1)} %bitcast.130) | data formatting | bytes 4194304
  79.8 5.2 %all-to-all-start = ((f32[64,8,8,128]{3,2,1,0:T(8,128)}), f32[64,8,8,128]{3,2,1,0:T(8,128)}, u32[]{:S(2)}, u32[]{:S(2)}) async-start(f32[64,8,8,128]{3,2,1,0:T(8,128)} %bitcast.12), calls=%async_computation | async-start | bytes 4194304 | tf_op jit(solution)/shard_map/all_to_all | solution.py:82
  85.3 0.9 fusion.68
  86.2 1.3 fusion.67
  87.4 1.6 %fusion.60 = (bf16[16,8,8,64]{3,2,1,0:T(8,128)(2,1)}, f32[16,8,8]{2,1,0:T(8,128)}) fusion(f32[16,8,8,64]{3,2,1,0:T(8,128)S(1)} %get-tuple-element.179, f32[16,8,8]{2,1,0:T(8,128)S(1)} %get-tuple-element.178), kind=kLoop, calls=%fused_computation.54 | loop fusion | flops 195584 | bytes 401408 | tf_op jit(solution)/shard_map/convert_element_type | solution.py:127
  92.0 1.7 %fusion.65 = (bf16[1,4,128,1024]{3,2,1,0:T(8,128)(2,1)S(1)}, bf16[1,4,128,1024]{3,2,1,0:T(8,128)(2,1)S(1)}) fusion(bf16[2,4,128,1024]{3,2,1,0:T(8,128)(2,1)} %all-gather.5.cloned.1.call-done), kind=kLoop, calls=%fused_computation.79 | loop fusion | bytes 4194304 | tf_op jit(solution)/shard_map/slice | solution.py:103
  94.7 1.3 fusion.66
  96.0 1.5 %copy.133 = f32[16,8,8]{2,1,0:T(8,128)} copy(f32[16,8,8]{0,2,1:T(8,128)} %get-tuple-element.176) | data formatting | bytes 8192 | tf_op jit(solution)/shard_map/reduce_max | solution.py:18
  97.5 1.6 %exponential_multiply_fusion = (f32[16,8,8]{2,1,0:T(8,128)}, f32[16,8,8]{2,1,0:T(8,128)}, f32[16,8,8]{2,1,0:T(8,128)}, f32[16,8,8]{2,1,0:T(8,128)}) fusion(f32[16,8,8]{2,1,0:T(8,128)} %copy.133, f32[16,8,8]{2,1,0:T(8,128)S(1)} %reduce_max.36), kind=kLoop, calls=%fused_computation.72 | loop fusion | flops 6144 | bytes 24576 | tf_op jit(solution)/shard_map/mul;broadcast_in_dim | solution.py:38
  99.0 1.5 %copy.139 = f32[16,8,8]{0,2,1:T(8,128)} copy(f32[16,8,8]{2,1,0:T(8,128)} %get-tuple-element.174) | data formatting | bytes 8192 | tf_op jit(solution)/shard_map/jit(_where)/select_n | solution.py:35
  100.6 2.7 %fusion.25 = (f32[16,8,8]{0,2,1:T(8,128)}, bf16[16,8,8,512]{3,0,2,1:T(8,128)(2,1)}) fusion(f32[16,8,8,512]{3,0,2,1:T(8,128)S(1)} %get-tuple-element.177, f32[16,8,8]{0,2,1:T(8,128)} %copy.139), kind=kLoop, calls=%fused_computation.32 | loop fusion | flops 1571840 | bytes 3153920 | tf_op jit(solution)/shard_map/reduce_sum | solution.py:21
  103.3 0.8 copy.156
  104.1 1.1 multiply_add_fusion
  105.3 0.9 copy.138
  106.1 0.9 copy.143
  107.4 25.0 %all-to-all-done = f32[64,8,8,128]{3,2,1,0:T(8,128)} async-done(((f32[64,8,8,128]{3,2,1,0:T(8,128)}), f32[64,8,8,128]{3,2,1,0:T(8,128)}, u32[]{:S(2)}, u32[]{:S(2)}) %all-to-all-start) | async-done | bytes 2097184 | tf_op jit(solution)/shard_map/all_to_all | solution.py:82
  132.4 2.0 %multiply_reduce_fusion = f32[16,8,8,128]{3,2,1,0:T(8,128)S(1)} fusion(f32[4,16,8,8,128]{4,3,2,1,0:T(8,128)} %bitcast.13, f32[4,16,8,8]{3,2,1,0:T(8,128)S(1)} %subtract_exponential_fusion.2), kind=kLoop, calls=%fused_computation.31 | loop fusion | flops 917504 | bytes 2637824 | tf_op jit(solution)/shard_map/reduce_sum | solution.py:49
  134.4 1.5 %fusion.52 = f32[16,8,8,128]{3,2,0,1:T(8,128)S(1)} fusion(bf16[512,8,128,1]{2,1,0,3:T(8,128)(2,1)S(1)} %bitcast.142, bf16[16,8,8,512]{3,0,2,1:T(8,128)(2,1)S(1)} %copy-done.2, f32[16,8,8,128]{3,2,1,0:T(8,128)S(1)} %multiply_reduce_fusion, f32[16,8,8]{2,0,1:T(8,128)S(1)} %copy.147, f32[16,8,8]{2,0,1:T(8,128)S(1)} %copy.145, f32[16,8,8]{2,0,1:T(8,128)S(1)} %copy.143, ...), kind=kOutput, calls=%fused_computation.46 | convolution fusion | flops 135004160 | bytes 3166208 | tf_op jit(solution)/shard_map/bhgt,thd->bhgd/dot_general | solution.py:22
  136.0 1.0 fusion.53
  137.0 0.9 copy.247
  (97 shorter events, 12.4 us)
Async XLA Ops:
  6.5 33.1 %all-gather.3.cloned.1.call-start = ((), (), s32[]{:S(2)}) async-start(), calls=%async_computation.3 | async-start | bytes 1310720 | tf_op jit(solution)/shard_map/all_gather | solution.py:66
  7.3 84.8 %all-gather.5.cloned.1.call-start = ((), (), s32[]{:S(2)}) async-start(), calls=%async_computation.4 | async-start | bytes 2621440 | tf_op jit(solution)/shard_map/all_gather | solution.py:98
  21.6 3.9 %copy-start.10 = (s32[16]{0:T(128)S(1)}, s32[16]{0:T(128)}, u32[]{:S(2)}) copy-start(s32[16]{0:T(128)} %param.21) | copy-start | bytes 196
  21.6 3.9 %copy-start.13 = (s32[4]{0:T(128)S(1)}, s32[4]{0:T(128)}, u32[]{:S(2)}) copy-start(s32[4]{0:T(128)} %param.20) | copy-start | bytes 52
  41.9 1.6 %copy-start = (bf16[1024,8,128]{2,0,1:T(8,128)(2,1)S(1)}, bf16[1024,8,128]{2,0,1:T(8,128)(2,1)}, u32[]{:S(2)}) copy-start(bf16[1024,8,128]{2,0,1:T(8,128)(2,1)} %get-tuple-element.296) | copy-start | bytes 6291460 | tf_op jit(solution)/shard_map/while
  46.2 1.7 %copy-start = (bf16[1024,8,128]{2,0,1:T(8,128)(2,1)S(1)}, bf16[1024,8,128]{2,0,1:T(8,128)(2,1)}, u32[]{:S(2)}) copy-start(bf16[1024,8,128]{2,0,1:T(8,128)(2,1)} %get-tuple-element.296) | copy-start | bytes 6291460 | tf_op jit(solution)/shard_map/while
  50.6 1.6 %copy-start = (bf16[1024,8,128]{2,0,1:T(8,128)(2,1)S(1)}, bf16[1024,8,128]{2,0,1:T(8,128)(2,1)}, u32[]{:S(2)}) copy-start(bf16[1024,8,128]{2,0,1:T(8,128)(2,1)} %get-tuple-element.296) | copy-start | bytes 6291460 | tf_op jit(solution)/shard_map/while
  54.8 1.6 %copy-start = (bf16[1024,8,128]{2,0,1:T(8,128)(2,1)S(1)}, bf16[1024,8,128]{2,0,1:T(8,128)(2,1)}, u32[]{:S(2)}) copy-start(bf16[1024,8,128]{2,0,1:T(8,128)(2,1)} %get-tuple-element.296) | copy-start | bytes 6291460 | tf_op jit(solution)/shard_map/while
  59.1 9.0 %all-to-all-start.1 = ((f32[4,1,1024]{2,1,0:T(1,128)}), f32[4,1,1024]{2,1,0:T(1,128)S(1)}, u32[]{:S(2)}, u32[]{:S(2)}) async-start(f32[4,1,1024]{2,1,0:T(1,128)} %reshape.165), calls=%async_computation.1 | async-start | bytes 32768 | tf_op jit(solution)/shard_map/all_to_all | solution.py:83
  62.3 5.0 %copy-start.7 = (f32[4,16,8,8]{3,2,1,0:T(8,128)S(1)}, f32[4,16,8,8]{3,2,1,0:T(8,128)}, u32[]{:S(2)}) copy-start(f32[4,16,8,8]{3,2,1,0:T(8,128)} %get-tuple-element.74) | copy-start | bytes 49156
  62.3 10.8 %copy-start.8 = (bf16[2,16,1024]{2,1,0:T(8,128)(2,1)S(1)}, bf16[2,16,1024]{2,1,0:T(8,128)(2,1)}, u32[]{:S(2)}) copy-start(bf16[2,16,1024]{2,1,0:T(8,128)(2,1)} %param.15) | copy-start | bytes 196612
  62.4 10.8 %copy-start.5 = (bf16[16,8192]{1,0:T(8,128)(2,1)S(1)}, bf16[16,8192]{1,0:T(8,128)(2,1)}, u32[]{:S(2)}) copy-start(bf16[16,8192]{1,0:T(8,128)(2,1)} %param.14) | copy-start | bytes 786436
  68.1 11.6 %all-to-all-start.2 = ((f32[4,1,1024]{2,1,0:T(1,128)}), f32[4,1,1024]{2,1,0:T(1,128)S(1)}, u32[]{:S(2)}, u32[]{:S(2)}) async-start(f32[4,1,1024]{2,1,0:T(1,128)} %reshape.167), calls=%async_computation.2 | async-start | bytes 32768 | tf_op jit(solution)/shard_map/all_to_all | solution.py:84
  73.2 13.0 %copy-start.3 = (bf16[2,8,64,128]{3,2,1,0:T(8,128)(2,1)}, bf16[2,8,64,128]{3,2,1,0:T(8,128)(2,1)S(1)}, u32[]{:S(2)}) copy-start(bf16[2,8,64,128]{3,2,1,0:T(8,128)(2,1)S(1)} %copy.193) | copy-start | bytes 786436
  79.8 5.2 %copy-start.11 = (s32[4]{0:T(128)S(1)}, s32[4]{0:T(128)}, u32[]{:S(2)}) copy-start(s32[4]{0:T(128)} %param.19) | copy-start | bytes 52
  79.8 5.3 %copy-start.12 = (s32[16]{0:T(128)S(1)}, s32[16]{0:T(128)}, u32[]{:S(2)}) copy-start(s32[16]{0:T(128)} %param.17) | copy-start | bytes 196
  79.8 52.6 %all-to-all-start = ((f32[64,8,8,128]{3,2,1,0:T(8,128)}), f32[64,8,8,128]{3,2,1,0:T(8,128)}, u32[]{:S(2)}, u32[]{:S(2)}) async-start(f32[64,8,8,128]{3,2,1,0:T(8,128)} %bitcast.12), calls=%async_computation | async-start | bytes 4194304 | tf_op jit(solution)/shard_map/all_to_all | solution.py:82
  93.7 1.0 copy-start.4
  107.3 27.1 %copy-start.2 = (bf16[16,8,8,512]{3,0,2,1:T(8,128)(2,1)S(1)}, bf16[16,8,8,512]{3,0,2,1:T(8,128)(2,1)}, u32[]{:S(2)}) copy-start(bf16[16,8,8,512]{3,0,2,1:T(8,128)(2,1)} %get-tuple-element.165) | copy-start | bytes 3145732
  134.4 1.6 %copy-start.1 = (bf16[128,8,8,128]{3,2,1,0:T(8,128)(2,1)S(1)}, bf16[128,8,8,128]{3,2,1,0:T(8,128)(2,1)}, u32[]{:S(2)}) copy-start(bf16[128,8,8,128]{3,2,1,0:T(8,128)(2,1)} %copy.196) | copy-start | bytes 6291460
  134.4 1.6 %copy-start.6 = (bf16[16,8,8,64]{3,2,1,0:T(8,128)(2,1)S(1)}, bf16[16,8,8,64]{3,2,1,0:T(8,128)(2,1)}, u32[]{:S(2)}) copy-start(bf16[16,8,8,64]{3,2,1,0:T(8,128)(2,1)} %get-tuple-element.168) | copy-start | bytes 393220
  134.4 1.6 %copy-start.9 = (f32[16,8,128]{2,0,1:T(8,128)S(1)}, f32[16,8,128]{2,0,1:T(8,128)}, u32[]{:S(2)}) copy-start(f32[16,8,128]{2,0,1:T(8,128)} %copy.152) | copy-start | bytes 196612
Sparse Core Ops, SparseCore 0:
  8.9 30.6 all-gather.2
  41.2 22.0 all-gather.4
where the time goes:
time: 146 us; the launch traced here: 145 us
  local copies, waits for them, and re-layouts  49.2 us (34%)
  waiting for transfers between devices  40 us (27%)
  other arithmetic  15 us (10%)
  between operations  13.8 us (9%)
  starting transfers between devices  13.5 us (9%)
  matrix products  13.1 us (9%)
    all_to_all x1, waiting for transfers between devices, on_device(): lax.all_to_all(held_mixed, 'ctx', split_axis=0, concat_axis=0, tiled=True)  25 us
    unnamed x40, local copies, waits for them, and re-layouts  17.8 us
    all_gather x1, waiting for transfers between devices, on_device(): query_rows = lax.all_gather(queries, 'ctx', axis=0, tiled=True)  13.6 us
    while x2, local copies, waits for them, and re-layouts, on_device(): mixed, maxima, totals = lax.map(one_block, blocks)  6.96 us
    dynamic_update_slice x8, local copies, waits for them, and re-layouts, on_device(): mixed, maxima, totals = lax.map(one_block, blocks)  6.15 us
    reduce_sum x5, other arithmetic, attend(): totals = jnp.sum(weights, axis=-1)  6.14 us
    dot_general x5, matrix products, attend(): jnp.einsum('bhgt,thd->bhgd', weights.astype(jnp.bfloat16), value_rows, pr...  5.48 us
    all_to_all x1, starting transfers between devices, on_device(): lax.all_to_all(held_mixed, 'ctx', split_axis=0, concat_axis=0, tiled=True)  5.22 us
  transfers between devices with their start and end apart: 5, of which 2 were waited for; matrix products, arithmetic and copies ran while one was open for 49% of the time, Pallas kernels for 0%

commit v1 on v0

--- a/solution.py
+++ b/solution.py
@@ -1,3 +1,4 @@
+import functools
 import math
 import jax
 import jax.numpy as jnp
@@ -8,6 +9,34 @@
 KV_HEADS = 8
 HEAD_DIM = 128
 NODE_LEN = 128
+
+
+def mix_quarters(sheet, axis_no, point):
+    carry_out, earlier = (sheet.shape[:axis_no], sheet.shape[axis_no + 1 :])
+    state_next = jnp.moveaxis(sheet.reshape(*carry_out, point, -1, *earlier), axis_no, 0)
+    return state_next
+
+
+def routes_all_map(my_data, dimension_no):
+    value_now = list(my_data.shape[1:])
+    value_now[dimension_no] *= my_data.shape[0]
+    y1 = jnp.moveaxis(my_data, 0, dimension_no).reshape(value_now)
+    return y1
+
+
+def divide_axis_part(array_in, group_axis, q_in, unit):
+    y_new, main = (lax.axis_size(group_axis), lax.axis_index(group_axis))
+    arr_next = mix_quarters(array_in, q_in, y_new)
+    fields = [arr_next[main]]
+    for j0 in range(1, y_new):
+        spare = arr_next[main ^ j0]
+        fields.append(lax.ppermute(spare, group_axis, [(it, it ^ j0) for it in range(y_new)]))
+    arr_next = jnp.stack(fields, axis=0)[main ^ jnp.arange(y_new)]
+    k_now = routes_all_map(arr_next, unit)
+    return k_now
+
+
+body_form = functools.partial(divide_axis_part, group_axis="ctx", q_in=0, unit=0)
 
 
 def attend(query_block, key_rows, value_rows, live_mask):
@@ -81,7 +110,7 @@
     back_mixed, back_maxima, back_totals = (
         lax.all_to_all(held_mixed, "ctx", split_axis=0, concat_axis=0, tiled=True),
         lax.all_to_all(held_maxima, "ctx", split_axis=0, concat_axis=0, tiled=True),
-        lax.all_to_all(held_totals, "ctx", split_axis=0, concat_axis=0, tiled=True),
+        body_form(held_totals),
     )
     prefix_state = merge_parts(back_mixed, back_maxima, back_totals, ctx_size, rollouts, group)
 

time: 146 us -> 158 us (1.082)
  local copies, waits for them, and re-layouts: 49.2 us -> 61.3 us
  waiting for transfers between devices: 40 us -> 48.1 us
  other arithmetic: 15 us -> 8.62 us
  starting transfers between devices: 13.5 us -> 11.6 us
    ppermute x0 -> x3, waiting for transfers between devices: none -> 36.7 us  [divide_axis_part(): lax.ppermute(spare, group_axis, [(it, it ^ j0) for it in range(y_new)])]
    all_to_all x1, waiting for transfers between devices: 25 us -> 0.01 us  [on_device(): lax.all_to_all(held_mixed, 'ctx', split_axis=0, concat_axis=0, tiled=True)]
    all_gather x1, waiting for transfers between devices: 13.6 us -> 7.2 us  [on_device(): query_rows = lax.all_gather(queries, 'ctx', axis=0, tiled=True)]
    all_to_all x1 -> x0, starting transfers between devices: 5.03 us -> none  [on_device(): lax.all_to_all(held_totals, 'ctx', split_axis=0, concat_axis=0, tiled=True)]
    ppermute x0 -> x3, starting transfers between devices: none -> 4.42 us  [divide_axis_part(): lax.ppermute(spare, group_axis, [(it, it ^ j0) for it in range(y_new)])]
    exp x3, local copies, waits for them, and re-layouts: 0.04 us -> 3.62 us  [combine(): scale_a = jnp.exp(maxima_a - anchor)]
    while x8, local copies, waits for them, and re-layouts: 0.36 us -> 3.3 us
    all_to_all x1, waiting for transfers between devices: 0.01 us -> 2.72 us  [on_device(): lax.all_to_all(held_maxima, 'ctx', split_axis=0, concat_axis=0, tiled=True)]
  transfers between devices with their start and end apart: 5 -> 7, of which waited for: 2 -> 4; matrix products, arithmetic and copies ran while one was open for 49% -> 48% of each run, Pallas kernels for 0% -> 0%
where the time goes in v1:
time: 158 us; the launch traced here: 157 us
  local copies, waits for them, and re-layouts  61.3 us (39%)
  waiting for transfers between devices  48.1 us (30%)
  between operations  13.9 us (9%)
  matrix products  13.5 us (9%)
  starting transfers between devices  11.6 us (7%)
  other arithmetic  8.62 us (5%)
    ppermute x3, waiting for transfers between devices, divide_axis_part(): lax.ppermute(spare, group_axis, [(it, it ^ j0) for it in range(y_new)])  36.7 us
    unnamed x71, local copies, waits for them, and re-layouts  18.6 us
    dynamic_update_slice x12, local copies, waits for them, and re-layouts, on_device(): mixed, maxima, totals = lax.map(one_block, blocks)  8.61 us
    all_gather x1, waiting for transfers between devices, on_device(): query_rows = lax.all_gather(queries, 'ctx', axis=0, tiled=True)  7.2 us
    while x3, local copies, waits for them, and re-layouts, on_device(): mixed, maxima, totals = lax.map(one_block, blocks)  7.08 us
    dot_general x5, matrix products, attend(): jnp.einsum('bhgt,thd->bhgd', weights.astype(jnp.bfloat16), value_rows, pr...  5.49 us
    reduce_sum x5, other arithmetic, attend(): totals = jnp.sum(weights, axis=-1)  4.83 us
    ppermute x3, starting transfers between devices, divide_axis_part(): lax.ppermute(spare, group_axis, [(it, it ^ j0) for it in range(y_new)])  4.42 us
  transfers between devices with their start and end apart: 7, of which 4 were waited for; matrix products, arithmetic and copies ran while one was open for 48% of the time, Pallas kernels for 0%

profile of v1, /device:TPU:0, one launch (start us, length us, event | category | flops | bytes accessed | tf_op | source)
XLA Modules:
  0.0 157.1 jit_solution(14423607416140186390)
XLA Ops:
  8.0 4.0 %fusion.65 = (bf16[1,1024,1024]{2,1,0:T(8,128)(2,1)}, bf16[1,1024,1024]{2,1,0:T(8,128)(2,1)S(1)}) fusion(bf16[2,1024,1024]{2,1,0:T(8,128)(2,1)} %param.13), kind=kLoop, calls=%fused_computation.88 | loop fusion | bytes 8388608 | tf_op jit(solution)/shard_map/slice | solution.py:90
  12.0 2.6 %copy.185 = bf16[1,1024,1024]{1,2,0:T(8,128)(2,1)} copy(bf16[1,1024,1024]{2,1,0:T(8,128)(2,1)S(1)} %get-tuple-element.163) | data formatting | bytes 4194304
  14.6 3.0 %copy.126 = bf16[1024,8,128]{2,0,1:T(8,128)(2,1)S(1)} copy(bf16[1024,8,128]{0,2,1:T(8,128)(2,1)} %bitcast.141) | data formatting | bytes 4194304 | tf_op jit(solution)/shard_map/while | solution.py:103
  17.6 4.0 %copy.186 = bf16[1,1024,1024]{1,2,0:T(8,128)(2,1)} copy(bf16[1,1024,1024]{2,1,0:T(8,128)(2,1)} %get-tuple-element.162) | data formatting | bytes 4194304
  21.6 3.9 %copy.127 = bf16[1024,8,128]{2,0,1:T(8,128)(2,1)} copy(bf16[1024,8,128]{0,2,1:T(8,128)(2,1)} %bitcast.142) | data formatting | bytes 4194304 | tf_op jit(solution)/shard_map/while | solution.py:103
  26.1 4.2 %fusion.64 = (bf16[1,16,64,1024]{3,2,1,0:T(8,128)(2,1)}, bf16[1,16,64,1024]{3,2,1,0:T(8,128)(2,1)S(1)}) fusion(bf16[2,16,64,1024]{3,2,1,0:T(8,128)(2,1)} %param.16), kind=kLoop, calls=%fused_computation.87 | loop fusion | bytes 8388608 | tf_op jit(solution)/shard_map/slice | solution.py:144
  30.3 2.0 %copy.196 = bf16[128,8,8,128]{3,2,1,0:T(8,128)(2,1)} copy(bf16[128,8,8,128]{3,1,2,0:T(8,128)(2,1)S(1)} %bitcast.144) | data formatting | bytes 4194304
  32.4 7.2 %all-gather.3.cloned.1.call-done = bf16[64,8192]{1,0:T(8,128)(2,1)} async-done(((bf16[16,8192]{1,0:T(8,128)(2,1)}), bf16[64,8192]{1,0:T(8,128)(2,1)}) %all-gather.3.cloned.1.call-update) | async-done | bytes 1048592 | tf_op jit(solution)/shard_map/all_gather | solution.py:95
  39.6 1.5 copy.191
  41.1 22.6 %while.27 = (s32[]{:T(128)}, f32[4,16,8,8,128]{4,3,2,1,0:T(8,128)}, f32[4,16,8,8]{3,2,1,0:T(8,128)}, f32[4,16,8,8]{3,1,2,0:T(8,128)}, bf16[4,16,8,8,128]{4,3,2,1...) while((s32[]{:T(128)}, f32[4,16,8,8,128]{4,3,2,1,0:T(8,128)}, ...), condition=%wide.region_3.4_spmd, body=%wide.region_0.3_spmd.sunk | while | flops 545259520 | bytes 27166324 | solution.py:103
  41.1 0.8 bitcast_reduce_fusion.2
  42.7 1.0 fusion.81
  43.7 0.9 copy_dynamic-update-slice_fusion.4
  44.6 0.9 fusion.82
  47.6 0.9 copy-done
  48.5 1.0 fusion.81
  49.5 0.9 copy_dynamic-update-slice_fusion.4
  50.3 0.9 fusion.82
  52.5 0.8 bitcast_reduce_fusion.2
  53.3 0.8 copy-done
  54.1 1.0 fusion.81
  55.1 0.9 copy_dynamic-update-slice_fusion.4
  55.9 0.9 fusion.82
  58.9 0.8 copy-done
  59.7 1.0 fusion.81
  60.7 0.9 copy_dynamic-update-slice_fusion.4
  61.6 0.9 fusion.82
  63.7 1.7 %reshape.181 = f32[4,1,1024]{2,1,0:T(1,128)} reshape(f32[64,8,8]{2,1,0:T(8,128)} %bitcast.14) | data formatting | bytes 32768
  65.4 3.2 %all-to-all-start.1 = ((f32[4,1,1024]{2,1,0:T(1,128)}), f32[4,1,1024]{2,1,0:T(1,128)S(1)}, u32[]{:S(2)}, u32[]{:S(2)}) async-start(f32[4,1,1024]{2,1,0:T(1,128)} %reshape.181), calls=%async_computation.1 | async-start | bytes 32768 | tf_op jit(solution)/shard_map/all_to_all | solution.py:112
  68.6 2.9 %fusion.68 = (f32[16,8,8]{2,1,0:T(8,128)S(1)}, f32[16,8,8,64]{3,2,1,0:T(8,128)S(1)}) fusion(bf16[16,8,8,128]{3,2,1,0:T(8,128)(2,1)S(1)} %bitcast.152, bf16[16,64,8,128]{3,2,1,0:T(8,128)(2,1)} %bitcast.139, pred[16,64]{1,0:T(8,128)(4,1)S(1)} %iota_compare_fusion.1), kind=kOutput, calls=%fused_computation.91 | convolution fusion | flops 16972800 | bytes 2626560 | tf_op jit(solution)/shard_map/rhgd,rshd->rhgs/dot_general | solution.py:146
  71.5 2.7 %all-to-all-done.1 = f32[4,1,1024]{2,1,0:T(1,128)S(1)} async-done(((f32[4,1,1024]{2,1,0:T(1,128)}), f32[4,1,1024]{2,1,0:T(1,128)S(1)}, u32[]{:S(2)}, u32[]{:S(2)}) %all-to-all-start.1) | async-done | bytes 16416 | tf_op jit(solution)/shard_map/all_to_all | solution.py:112
  74.2 3.9 %all-to-all-start = ((f32[64,8,8,128]{3,2,1,0:T(8,128)}), f32[64,8,8,128]{3,2,1,0:T(8,128)S(1)}, u32[]{:S(2)}, u32[]{:S(2)}) async-start(f32[64,8,8,128]{3,2,1,0:T(8,128)} %bitcast.151), calls=%async_computation | async-start | bytes 4194304 | tf_op jit(solution)/shard_map/all_to_all | solution.py:111
  78.2 0.9 fusion.60
  81.6 3.6 %copy.197 = bf16[128,8,8,128]{3,2,1,0:T(8,128)(2,1)} copy(bf16[128,8,8,128]{3,1,2,0:T(8,128)(2,1)} %bitcast.143) | data formatting | bytes 4194304
  86.3 1.8 %collective-permute-start = (f32[16,8,8]{0,2,1:T(8,128)S(1)}, f32[16,8,8]{0,2,1:T(8,128)S(1)}, u32[]{:S(2)}, u32[]{:S(2)}) collective-permute-start(f32[16,8,8]{0,2,1:T(8,128)S(1)} %bitcast.161), channel_id=1, source_target_pairs={{0,4},{4,0},{8,12},{12,8},{1,5},{5,1},{9,13},{13,9},{2,6},{6,2},{1... | collective-permute-start | bytes 12296 | tf_op jit(solution)/shard_map/ppermute | solution.py:33
  88.2 2.4 %collective-permute-start.1 = (f32[16,8,8]{0,2,1:T(8,128)S(1)}, f32[16,8,8]{0,2,1:T(8,128)S(1)}, u32[]{:S(2)}, u32[]{:S(2)}) collective-permute-start(f32[16,8,8]{0,2,1:T(8,128)S(1)} %bitcast.162), channel_id=1, source_target_pairs={{0,8},{4,12},{8,0},{12,4},{1,9},{5,13},{9,1},{13,5},{2,10},{6,14},... | collective-permute-start | bytes 12296 | tf_op jit(solution)/shard_map/ppermute | solution.py:33
  90.8 21.6 %collective-permute-done = f32[16,8,8]{0,2,1:T(8,128)S(1)} collective-permute-done((f32[16,8,8]{0,2,1:T(8,128)S(1)}, f32[16,8,8]{0,2,1:T(8,128)S(1)}, u32[]{:S(2)}, u32[]{:S(2)}) %collective-permute-start) | collective-permute-done | bytes 4128 | tf_op jit(solution)/shard_map/ppermute | solution.py:33
  112.4 15.1 %collective-permute-done.1 = f32[16,8,8]{0,2,1:T(8,128)S(1)} collective-permute-done((f32[16,8,8]{0,2,1:T(8,128)S(1)}, f32[16,8,8]{0,2,1:T(8,128)S(1)}, u32[]{:S(2)}, u32[]{:S(2)}) %collective-permute-start.1) | collective-permute-done | bytes 4128 | tf_op jit(solution)/shard_map/ppermute | solution.py:33
  129.8 0.8 copy.133
  130.7 1.7 %fusion.66 = (bf16[1,4,128,1024]{3,2,1,0:T(8,128)(2,1)S(1)}, bf16[1,4,128,1024]{3,2,1,0:T(8,128)(2,1)S(1)}) fusion(bf16[2,4,128,1024]{3,2,1,0:T(8,128)(2,1)} %all-gather.5.cloned.1.call-done), kind=kLoop, calls=%fused_computation.89 | loop fusion | bytes 4194304 | tf_op jit(solution)/shard_map/slice | solution.py:132
  133.4 1.4 fusion.25
  135.6 1.5 copy.137
  137.0 1.5 copy.143
  138.5 1.5 copy.146
  141.3 1.2 copy.195
  146.7 1.5 fusion.52
  148.3 1.0 fusion.53
  149.4 0.9 copy.247
  (146 shorter events, 23.4 us)
Async XLA Ops:
  6.5 33.1 %all-gather.3.cloned.1.call-start = ((), (), s32[]{:S(2)}) async-start(), calls=%async_computation.2 | async-start | bytes 1310720 | tf_op jit(solution)/shard_map/all_gather | solution.py:95
  7.3 123.4 %all-gather.5.cloned.1.call-start = ((), (), s32[]{:S(2)}) async-start(), calls=%async_computation.3 | async-start | bytes 2621440 | tf_op jit(solution)/shard_map/all_gather | solution.py:127
  21.6 4.0 %copy-start.4 = (bf16[16,8192]{1,0:T(8,128)(2,1)S(1)}, bf16[16,8192]{1,0:T(8,128)(2,1)}, u32[]{:S(2)}) copy-start(bf16[16,8192]{1,0:T(8,128)(2,1)} %param.14) | copy-start | bytes 786436
  21.6 4.0 %copy-start.26 = (s32[16]{0:T(128)S(1)}, s32[16]{0:T(128)}, u32[]{:S(2)}) copy-start(s32[16]{0:T(128)} %param.21) | copy-start | bytes 196
  21.6 4.0 %copy-start.29 = (s32[4]{0:T(128)S(1)}, s32[4]{0:T(128)}, u32[]{:S(2)}) copy-start(s32[4]{0:T(128)} %param.20) | copy-start | bytes 52
  30.3 2.0 %copy-start.27 = (s32[16]{0:T(128)S(1)}, s32[16]{0:T(128)}, u32[]{:S(2)}) copy-start(s32[16]{0:T(128)} %param.17) | copy-start | bytes 196
  41.1 1.6 %copy-start = (bf16[1024,8,128]{2,0,1:T(8,128)(2,1)S(1)}, bf16[1024,8,128]{2,0,1:T(8,128)(2,1)}, u32[]{:S(2)}) copy-start(bf16[1024,8,128]{2,0,1:T(8,128)(2,1)} %get-tuple-element.295) | copy-start | bytes 6291460 | tf_op jit(solution)/shard_map/while
  46.7 1.7 %copy-start = (bf16[1024,8,128]{2,0,1:T(8,128)(2,1)S(1)}, bf16[1024,8,128]{2,0,1:T(8,128)(2,1)}, u32[]{:S(2)}) copy-start(bf16[1024,8,128]{2,0,1:T(8,128)(2,1)} %get-tuple-element.295) | copy-start | bytes 6291460 | tf_op jit(solution)/shard_map/while
  52.5 1.6 %copy-start = (bf16[1024,8,128]{2,0,1:T(8,128)(2,1)S(1)}, bf16[1024,8,128]{2,0,1:T(8,128)(2,1)}, u32[]{:S(2)}) copy-start(bf16[1024,8,128]{2,0,1:T(8,128)(2,1)} %get-tuple-element.295) | copy-start | bytes 6291460 | tf_op jit(solution)/shard_map/while
  58.1 1.6 %copy-start = (bf16[1024,8,128]{2,0,1:T(8,128)(2,1)S(1)}, bf16[1024,8,128]{2,0,1:T(8,128)(2,1)}, u32[]{:S(2)}) copy-start(bf16[1024,8,128]{2,0,1:T(8,128)(2,1)} %get-tuple-element.295) | copy-start | bytes 6291460 | tf_op jit(solution)/shard_map/while
  65.4 8.8 %all-to-all-start.1 = ((f32[4,1,1024]{2,1,0:T(1,128)}), f32[4,1,1024]{2,1,0:T(1,128)S(1)}, u32[]{:S(2)}, u32[]{:S(2)}) async-start(f32[4,1,1024]{2,1,0:T(1,128)} %reshape.181), calls=%async_computation.1 | async-start | bytes 32768 | tf_op jit(solution)/shard_map/all_to_all | solution.py:112
  74.2 6.3 %copy-start.24 = (bf16[2,16,1024]{2,1,0:T(8,128)(2,1)S(1)}, bf16[2,16,1024]{2,1,0:T(8,128)(2,1)}, u32[]{:S(2)}) copy-start(bf16[2,16,1024]{2,1,0:T(8,128)(2,1)} %param.15) | copy-start | bytes 196612
  74.2 71.2 %all-to-all-start = ((f32[64,8,8,128]{3,2,1,0:T(8,128)}), f32[64,8,8,128]{3,2,1,0:T(8,128)S(1)}, u32[]{:S(2)}, u32[]{:S(2)}) async-start(f32[64,8,8,128]{3,2,1,0:T(8,128)} %bitcast.151), calls=%async_computation | async-start | bytes 4194304 | tf_op jit(solution)/shard_map/all_to_all | solution.py:111
  81.6 4.2 %copy-start.28 = (s32[4]{0:T(128)S(1)}, s32[4]{0:T(128)}, u32[]{:S(2)}) copy-start(s32[4]{0:T(128)} %param.19) | copy-start | bytes 52
  81.6 4.4 %copy-start.6 = (f32[4,16,8,8]{3,1,2,0:T(8,128)S(1)}, f32[4,16,8,8]{3,1,2,0:T(8,128)}, u32[]{:S(2)}) copy-start(f32[4,16,8,8]{3,1,2,0:T(8,128)} %get-tuple-element.74) | copy-start | bytes 49156
  86.3 26.2 %collective-permute-start = (f32[16,8,8]{0,2,1:T(8,128)S(1)}, f32[16,8,8]{0,2,1:T(8,128)S(1)}, u32[]{:S(2)}, u32[]{:S(2)}) collective-permute-start(f32[16,8,8]{0,2,1:T(8,128)S(1)} %bitcast.161), channel_id=1, source_target_pairs={{0,4},{4,0},{8,12},{12,8},{1,5},{5,1},{9,13},{13,9},{2,6},{6,2},{1... | collective-permute-start | bytes 12296 | tf_op jit(solution)/shard_map/ppermute | solution.py:33
  88.2 39.4 %collective-permute-start.1 = (f32[16,8,8]{0,2,1:T(8,128)S(1)}, f32[16,8,8]{0,2,1:T(8,128)S(1)}, u32[]{:S(2)}, u32[]{:S(2)}) collective-permute-start(f32[16,8,8]{0,2,1:T(8,128)S(1)} %bitcast.162), channel_id=1, source_target_pairs={{0,8},{4,12},{8,0},{12,4},{1,9},{5,13},{9,1},{13,5},{2,10},{6,14},... | collective-permute-start | bytes 12296 | tf_op jit(solution)/shard_map/ppermute | solution.py:33
  90.6 37.0 %collective-permute-start.2 = (f32[16,8,8]{0,2,1:T(8,128)S(1)}, f32[16,8,8]{0,2,1:T(8,128)S(1)}, u32[]{:S(2)}, u32[]{:S(2)}) collective-permute-start(f32[16,8,8]{0,2,1:T(8,128)S(1)} %bitcast.163), channel_id=1, source_target_pairs={{0,12},{4,8},{8,4},{12,0},{1,13},{5,9},{9,5},{13,1},{2,14},{6,10},... | collective-permute-start | bytes 12296 | tf_op jit(solution)/shard_map/ppermute | solution.py:33
  133.4 1.5 copy-start.8
  133.4 1.4 copy-start.9
  133.4 1.4 copy-start.10
  134.8 10.6 %copy-start.5 = (f32[4,16,8,8]{3,2,1,0:T(8,128)S(1)}, f32[4,16,8,8]{3,2,1,0:T(8,128)}, u32[]{:S(2)}) copy-start(f32[4,16,8,8]{3,2,1,0:T(8,128)} %copy.133) | copy-start | bytes 49156
  135.6 8.5 %copy-start.12 = (f32[16,8,8]{0,2,1:T(8,128)S(1)}, f32[16,8,8]{0,2,1:T(8,128)}, u32[]{:S(2)}) copy-start(f32[16,8,8]{0,2,1:T(8,128)} %get-tuple-element.152) | copy-start | bytes 12292
  135.6 9.2 %copy-start.11 = (f32[16,8,8]{0,2,1:T(8,128)S(1)}, f32[16,8,8]{0,2,1:T(8,128)}, u32[]{:S(2)}) copy-start(f32[16,8,8]{0,2,1:T(8,128)} %get-tuple-element.149) | copy-start | bytes 12292
  140.6 2.7 %copy-start.13 = (f32[16,8,8]{0,2,1:T(8,128)S(1)}, f32[16,8,8]{0,2,1:T(8,128)}, u32[]{:S(2)}) copy-start(f32[16,8,8]{0,2,1:T(8,128)} %get-tuple-element.151) | copy-start | bytes 12292
  141.3 1.2 copy-start.14
  142.6 3.6 %copy-start.2 = (bf16[16,8,8,512]{3,0,2,1:T(8,128)(2,1)S(1)}, bf16[16,8,8,512]{3,0,2,1:T(8,128)(2,1)}, u32[]{:S(2)}) copy-start(bf16[16,8,8,512]{3,0,2,1:T(8,128)(2,1)} %get-tuple-element.165) | copy-start | bytes 3145732
  144.0 2.2 %copy-start.15 = (f32[16,8,8]{2,0,1:T(8,128)S(1)}, f32[16,8,8]{2,0,1:T(8,128)}, u32[]{:S(2)}) copy-start(f32[16,8,8]{2,0,1:T(8,128)} %copy.137) | copy-start | bytes 12292
  145.4 1.2 copy-start.3
  145.4 1.2 copy-start.16
  145.4 1.2 copy-start.17
  145.4 1.2 copy-start.19
  145.4 1.2 copy-start.22
  146.7 1.6 %copy-start.1 = (bf16[128,8,8,128]{3,2,1,0:T(8,128)(2,1)S(1)}, bf16[128,8,8,128]{3,2,1,0:T(8,128)(2,1)}, u32[]{:S(2)}) copy-start(bf16[128,8,8,128]{3,2,1,0:T(8,128)(2,1)} %copy.197) | copy-start | bytes 6291460
  146.7 1.6 %copy-start.7 = (bf16[16,8,8,64]{3,2,1,0:T(8,128)(2,1)S(1)}, bf16[16,8,8,64]{3,2,1,0:T(8,128)(2,1)}, u32[]{:S(2)}) copy-start(bf16[16,8,8,64]{3,2,1,0:T(8,128)(2,1)} %get-tuple-element.168) | copy-start | bytes 393220
  146.7 1.6 %copy-start.18 = (f32[16,8,8]{2,0,1:T(8,128)S(1)}, f32[16,8,8]{2,0,1:T(8,128)}, u32[]{:S(2)}) copy-start(f32[16,8,8]{2,0,1:T(8,128)} %copy.149) | copy-start | bytes 12292
  146.7 1.6 %copy-start.20 = (f32[16,8,8]{2,0,1:T(8,128)S(1)}, f32[16,8,8]{2,0,1:T(8,128)}, u32[]{:S(2)}) copy-start(f32[16,8,8]{2,0,1:T(8,128)} %copy.151) | copy-start | bytes 12292
  146.7 1.6 %copy-start.21 = (f32[16,8,8]{2,0,1:T(8,128)S(1)}, f32[16,8,8]{2,0,1:T(8,128)}, u32[]{:S(2)}) copy-start(f32[16,8,8]{2,0,1:T(8,128)} %copy.153) | copy-start | bytes 12292
  146.7 1.6 %copy-start.23 = (f32[16,8,8]{2,0,1:T(8,128)S(1)}, f32[16,8,8]{2,0,1:T(8,128)}, u32[]{:S(2)}) copy-start(f32[16,8,8]{2,0,1:T(8,128)} %copy.159) | copy-start | bytes 12292
  146.7 1.6 %copy-start.25 = (f32[16,8,128]{2,0,1:T(8,128)S(1)}, f32[16,8,128]{2,0,1:T(8,128)}, u32[]{:S(2)}) copy-start(f32[16,8,128]{2,0,1:T(8,128)} %copy.152) | copy-start | bytes 196612
Sparse Core Ops, SparseCore 0:
  8.9 30.6 all-gather.2
  41.1 22.1 all-gather.4
